TPU v7x, 32 devices: a whole 2x2x4 slice. The times are simulated.
32 devices in a mesh: groups: 1, row: 8 (over z, y), col: 4 (over x, core).
Axes of the slice: x: 2, y: 2, z: 4, core: 2. Of those that a mesh axis runs over, the one named last changes fastest.
Arguments:
- activations: bfloat16 [1024, 16384], P('groups', ('row', 'col')), may hold values from -2.5 to 2.5
- token_ids: int32 [1024], P('groups'), may hold values from 0 to 128255
- initial: float32 [16384, 256], P(('groups', 'row', 'col')), may hold values from -6 to 6
- block_mask: int32 [128, 2], P('groups'), may hold values 0 or 1
Outputs:
- gram: float32 [8, 4, 512, 16384], P('groups', 'col', None, 'row')
- repaired: float32 [16384, 256], P(('groups', 'row', 'col'))
All inputs are finite; a program needn't handle non-finite values.
Results may differ from a plain program's by a relative error of at most 0.0003.
Values may be sent and summed in bfloat16 or wider, within the bound.
No kernel may reach another device: no remote copies, remote signals or barrier semaphores. Data moves between devices by JAX's collectives and lax.ppermute only.
A program may use at most 128 MiB of HBM per device.

v0:
```python
import math
import jax
import jax.numpy as jnp
from jax import lax
from jax.sharding import PartitionSpec as P

D = 16384
ROWS = 1024
BLOCK = 128
ITERS = 2


def shards(activations, token_ids, initial, block_mask):
    matches = (token_ids[:, None] == token_ids[None, :]).astype(jnp.float32)
    weights = 1.0 / jnp.sum(matches, axis=1)
    weighted = (activations.astype(jnp.float32) * weights[:, None]).astype(jnp.bfloat16)
    column_panel = lax.all_gather(activations, "col", axis=1, tiled=True)
    gram_tile = lax.dot_general(
        lax.all_gather(weighted, "row", axis=1, tiled=True),
        column_panel,
        (((0,), (0,)), ((), ())),
        preferred_element_type=jnp.float32,
    ) * (1.0 / ROWS)
    shard_rows = initial.shape[0]
    col_count = lax.axis_size("col")
    first_feature = (lax.axis_index("row") * col_count + lax.axis_index("col")) * shard_rows
    block_index = (first_feature + jnp.arange(shard_rows, dtype=jnp.int32)) // BLOCK
    selector = (
        block_index[:, None] == jnp.arange(block_mask.shape[0], dtype=jnp.int32)[None, :]
    ).astype(jnp.float32)
    mask_rows = jnp.dot(selector, block_mask.astype(jnp.float32), precision=lax.Precision.HIGHEST)
    mask_full = jnp.repeat(mask_rows, BLOCK, axis=1)
    step_size = ROWS / (D + 2.0 * math.sqrt(D * ROWS) + ROWS)
    current = mask_full * initial
    for iteration in range(ITERS):
        change_now = current - initial
        projected = jnp.dot(
            activations.astype(jnp.float32), change_now, precision=lax.Precision.HIGHEST
        )
        totals = lax.psum(projected, ("row", "col"))
        pulled = lax.dot_general(
            weighted.astype(jnp.float32),
            totals,
            (((0,), (0,)), ((), ())),
            precision=lax.Precision.HIGHEST,
        ) * (1.0 / ROWS)
        current = mask_full * (current - step_size * pulled)
    gram_out = gram_tile.reshape(lax.axis_size("row"), 1, shard_rows, gram_tile.shape[1])
    return (gram_out, current)


def solution(mesh):
    in_specs = (
        P("groups", ("row", "col")),
        P("groups"),
        P(("groups", "row", "col"), None),
        P("groups", None),
    )
    out_specs = (P("groups", "col", None, "row"), P(("groups", "row", "col"), None))
    return jax.shard_map(shards, mesh=mesh, in_specs=in_specs, out_specs=out_specs, check_vma=False)
```

profile of v0, /device:TPU:0, one launch (start us, length us, event | category | flops | bytes accessed | tf_op | source)
XLA Modules:
  0.0 426.7 jit_solution(2539099986985370560)
XLA Ops:
  8.0 0.0 copy-start
  8.0 0.0 copy-start.2
  8.0 0.0 all-reduce.3.cloned.1.call-start
  8.1 1.1 fusion.8
  9.2 0.6 broadcast_in_dim.2
  9.8 4.3 %convolution_bitcast_fusion.1 = f32[1024,256]{0,1:T(8,128)} fusion(bf16[1024,512]{1,0:T(8,128)(2,1)} %param.4, f32[512,256]{1,0:T(8,128)} %param.6, f32[64,8,2,128]{3,2,1,0:T(2,128)S(1)} %bitcast.25), kind=kOutput, calls=%fused_computation.4 | convolution fusion | flops 1610874880 | bytes 3145728 | tf_op jit(solution)/shard_map/dot_general | solution.py:37
  14.1 0.0 all-reduce.3.cloned.1.call-update
  14.1 0.0 all-reduce.5.cloned.1.call-start
  14.1 0.0 copy-done.2
  14.1 0.5 convert_reduce_fusion
  14.7 0.0 copy-done
  14.7 0.3 multiply_convert_fusion
  15.0 0.0 copy-start.1
  15.0 132.6 %all-reduce.3.cloned.1.call-done = f32[1024,256]{0,1:T(8,128)} async-done(((f32[1024,256]{0,1:T(8,128)}), f32[1024,256]{0,1:T(8,128)}) %all-reduce.3.cloned.1.call-update) | async-done | bytes 1048592 | tf_op jit(solution)/shard_map/psum | solution.py:40
  147.6 2.6 fusion.1
  150.3 3.9 convolution_bitcast_fusion
  154.1 0.0 all-reduce.5.cloned.1.call-update
  154.2 0.0 all-gather.5.cloned.1.call-start
  154.2 0.5 all-gather.5.cloned.1.call-update
  154.7 0.0 copy-done.1
  154.7 0.2 all-gather.3.cloned.1.call-start
  155.0 0.4 all-gather.3.cloned.1.call-update
  155.3 234.5 %all-reduce.5.cloned.1.call-done = f32[1024,256]{0,1:T(8,128)} async-done(((f32[1024,256]{0,1:T(8,128)}), f32[1024,256]{0,1:T(8,128)}) %all-reduce.5.cloned.1.call-update) | async-done | bytes 1048592 | tf_op jit(solution)/shard_map/psum | solution.py:40
  389.9 3.6 fusion.3
  393.5 0.0 all-gather.5.cloned.1.call-done
  393.5 0.0 all-gather.3.cloned.1.call-done
  393.5 25.8 %convolution_multiply_fusion = f32[4096,2048]{1,0:T(8,128)} fusion(bf16[1024,4096]{1,0:T(8,128)(2,1)} %all-gather.3.cloned.1.call-done, bf16[1024,2048]{1,0:T(8,128)(2,1)} %all-gather.5.cloned.1.call-done), kind=kOutput, calls=%fused_computation | convolution fusion | flops 17188257792 | bytes 46137344 | tf_op jit(solution)/shard_map/dot_general | solution.py:18
  (2 shorter events, 0.0 us)
Async XLA Ops:
  8.0 6.7 %copy-start = (bf16[1024,512]{1,0:T(8,128)(2,1)S(1)}, bf16[1024,512]{1,0:T(8,128)(2,1)}, u32[]{:S(2)}) copy-start(bf16[1024,512]{1,0:T(8,128)(2,1)} %param.4) | copy-start | bytes 3145732
  8.0 6.1 %copy-start.2 = (s32[1024]{0:T(1024)S(1)}, s32[1024]{0:T(1024)}, u32[]{:S(2)}) copy-start(s32[1024]{0:T(1024)} %param.5) | copy-start | bytes 12292
  8.0 139.6 %all-reduce.3.cloned.1.call-start = ((), (), s32[]{:S(2)}) async-start(), calls=%async_computation.2 | async-start | bytes 2097152 | tf_op jit(solution)/shard_map/psum | solution.py:40
  14.1 375.8 %all-reduce.5.cloned.1.call-start = ((), (), s32[]{:S(2)}) async-start(), calls=%async_computation.3 | async-start | bytes 2097152 | tf_op jit(solution)/shard_map/psum | solution.py:40
  15.0 139.7 %copy-start.1 = (bf16[1024,512]{1,0:T(8,128)(2,1)}, bf16[1024,512]{1,0:T(8,128)(2,1)S(1)}, u32[]{:S(2)}) copy-start(bf16[1024,512]{1,0:T(8,128)(2,1)S(1)} %multiply_convert_fusion) | copy-start | bytes 3145732
  154.2 239.3 %all-gather.5.cloned.1.call-start = ((), (), s32[]{:S(2)}) async-start(), calls=%async_computation.1 | async-start | bytes 5242880 | tf_op jit(solution)/shard_map/all_gather | solution.py:17
  154.7 238.7 %all-gather.3.cloned.1.call-start = ((), (), s32[]{:S(2)}) async-start(), calls=%async_computation | async-start | bytes 9437184 | tf_op jit(solution)/shard_map/all_gather | solution.py:19
Sparse Core Ops, SparseCore 0:
  14.2 133.3 all-reduce.2
  154.3 235.5 all-reduce.4
Sparse Core Ops, SparseCore 1:
  156.2 33.8 all-gather.4
  192.5 125.3 all-gather.2
where the time goes:
time: 427 us
  waiting for transfers between devices  368 us (86%)
  matrix products  41.3 us (10%)
  between operations  15.6 us (4%)
    psum x2, waiting for transfers between devices, shards(): totals = lax.psum(projected, ('row', 'col'))  367 us
    dot_general x1, matrix products, shards(): lax.dot_general(lax.all_gather(weighted, 'row', axis=1, tiled=True), colu...  25.8 us
  transfers between devices with their start and end apart: 4, of which 2 were waited for; matrix products, arithmetic and copies ran while one was open for 1% of the time, Pallas kernels for 0%

commit v1 on v0

--- a/solution.py
+++ b/solution.py
@@ -8,6 +8,11 @@
 ROWS = 1024
 BLOCK = 128
 ITERS = 2
+
+
+def summed_here(x, axis):
+    pieces = lax.all_gather(x, axis)
+    return jnp.sum(pieces, axis=0)
 
 
 def shards(activations, token_ids, initial, block_mask):
@@ -37,7 +42,7 @@
         projected = jnp.dot(
             activations.astype(jnp.float32), change_now, precision=lax.Precision.HIGHEST
         )
-        totals = lax.psum(projected, ("row", "col"))
+        totals = summed_here(projected, ("row", "col"))
         pulled = lax.dot_general(
             weighted.astype(jnp.float32),
             totals,

time: 427 us -> 615 us (1.44)
  waiting for transfers between devices: 368 us -> 486 us
  local copies, waits for them, and re-layouts: 0.62 us -> 58.1 us
  other arithmetic: 0.84 us -> 18.9 us
    psum x2 -> x0, waiting for transfers between devices: 367 us -> none  [shards(): totals = lax.psum(projected, ('row', 'col'))]
    all_gather x0 -> x2, waiting for transfers between devices: none -> 364 us  [summed_here(): pieces = lax.all_gather(x, axis)]
    all_gather x1, waiting for transfers between devices: 0.01 us -> 121 us  [shards(): lax.all_gather(weighted, 'row', axis=1, tiled=True)]
    unnamed x6 -> x8, local copies, waits for them, and re-layouts: 0.02 us -> 57.5 us
    reduce_sum x0 -> x2, other arithmetic: none -> 15.1 us  [summed_here(): return jnp.sum(pieces, axis=0)]
  transfers between devices with their start and end apart: 4 -> 4, of which waited for: 2 -> 3; matrix products, arithmetic and copies ran while one was open for 1% -> 11% of each run, Pallas kernels for 0% -> 0%
where the time goes in v1:
time: 615 us; the launch traced here: 614 us
  waiting for transfers between devices  486 us (79%)
  local copies, waits for them, and re-layouts  58.1 us (9%)
  matrix products  37.3 us (6%)
  other arithmetic  18.9 us (3%)
  between operations  13.9 us (2%)
    all_gather x2, waiting for transfers between devices, summed_here(): pieces = lax.all_gather(x, axis)  364 us
    all_gather x1, waiting for transfers between devices, shards(): lax.all_gather(weighted, 'row', axis=1, tiled=True)  121 us
    unnamed x8, local copies, waits for them, and re-layouts  57.5 us
    dot_general x1, matrix products, shards(): lax.dot_general(lax.all_gather(weighted, 'row', axis=1, tiled=True), colu...  25.8 us
    reduce_sum x2, other arithmetic, summed_here(): return jnp.sum(pieces, axis=0)  15.1 us
  transfers between devices with their start and end apart: 4, of which 3 were waited for; matrix products, arithmetic and copies ran while one was open for 11% of the time, Pallas kernels for 0%

profile of v1, /device:TPU:0, one launch (start us, length us, event | category | flops | bytes accessed | tf_op | source)
XLA Modules:
  0.0 614.3 jit_solution(12399034532560028950)
XLA Ops:
  7.2 0.0 all-gather.11.cloned.1.call-start
  7.2 1.0 fusion.8
  8.2 0.6 broadcast_in_dim.2
  8.8 4.2 convolution_bitcast_fusion.1
  13.0 0.0 all-gather.11.cloned.1.call-update
  13.1 0.0 all-gather.9.cloned.1.call-start
  13.1 0.7 all-gather.9.cloned.1.call-update
  13.8 0.0 all-gather.7.cloned.1.call-start
  13.9 1.3 convert_reduce_fusion
  15.2 2.5 multiply_convert_fusion
  17.7 0.0 all-gather.7.cloned.1.call-update
  17.7 0.0 all-gather.13.cloned.1.call-start
  17.7 193.5 %all-gather.11.cloned.1.call-done = f32[32768,256]{0,1:T(8,128)} async-done(((f32[1024,256]{0,1:T(8,128)}), f32[32768,256]{0,1:T(8,128)}) %all-gather.11.cloned.1.call-update) | async-done | bytes 33554448 | tf_op jit(solution)/shard_map/all_gather | solution.py:14
  211.3 28.8 %copy.14 = f32[32,8,32,1024]{3,2,1,0:T(8,128)S(1)} copy(f32[32,8,32,1024]{3,1,2,0:T(8,128)} %bitcast.35) | data formatting | bytes 67108864
  240.0 0.0 copy-start.1
  240.0 0.0 copy-start.2
  240.1 0.0 copy-start
  240.1 7.5 %bitcast_reduce_fusion.1 = f32[1024,256]{0,1:T(8,128)S(1)} fusion(f32[32,8,32,1024]{3,2,1,0:T(8,128)S(1)} %copy.14), kind=kLoop, calls=%fused_computation.1 | loop fusion | flops 8126464 | bytes 34603008 | tf_op jit(solution)/shard_map/reduce_sum | solution.py:15
  247.6 0.0 copy-done.1
  247.6 0.0 copy-done.2
  247.6 1.3 fusion.1
  248.9 0.0 copy-done
  248.9 2.9 convolution_bitcast_fusion
  251.8 0.0 all-gather.13.cloned.1.call-update
  251.8 0.0 all-gather.9.cloned.1.call-done
  251.8 121.2 %all-gather.7.cloned.1.call-done = bf16[1024,4096]{1,0:T(8,128)(2,1)} async-done(((bf16[1024,512]{1,0:T(8,128)(2,1)}), bf16[1024,4096]{1,0:T(8,128)(2,1)}) %all-gather.7.cloned.1.call-update) | async-done | bytes 8388624 | tf_op jit(solution)/shard_map/all_gather | solution.py:24
  373.1 25.8 %convolution_multiply_fusion = f32[4096,2048]{1,0:T(8,128)} fusion(bf16[1024,4096]{1,0:T(8,128)(2,1)} %all-gather.7.cloned.1.call-done, bf16[1024,2048]{1,0:T(8,128)(2,1)} %all-gather.9.cloned.1.call-done), kind=kOutput, calls=%fused_computation.2 | convolution fusion | flops 17188257792 | bytes 46137344 | tf_op jit(solution)/shard_map/dot_general | solution.py:23
  398.9 170.5 %all-gather.13.cloned.1.call-done = f32[32768,256]{0,1:T(8,128)} async-done(((f32[1024,256]{0,1:T(8,128)}), f32[32768,256]{0,1:T(8,128)}) %all-gather.13.cloned.1.call-update) | async-done | bytes 33554448 | tf_op jit(solution)/shard_map/all_gather | solution.py:14
  569.4 28.8 %copy.15 = f32[32,8,32,1024]{3,2,1,0:T(8,128)S(1)} copy(f32[32,8,32,1024]{3,1,2,0:T(8,128)} %bitcast.36) | data formatting | bytes 67108864
  598.2 7.6 %bitcast_reduce_fusion = f32[1024,256]{0,1:T(8,128)S(1)} fusion(f32[32,8,32,1024]{3,2,1,0:T(8,128)S(1)} %copy.15), kind=kLoop, calls=%fused_computation | loop fusion | flops 8126464 | bytes 34603008 | tf_op jit(solution)/shard_map/reduce_sum | solution.py:15
  605.7 2.1 fusion.3
  (2 shorter events, 0.0 us)
Async XLA Ops:
  7.2 204.1 %all-gather.11.cloned.1.call-start = ((), (), s32[]{:S(2)}) async-start(), calls=%async_computation.2 | async-start | bytes 34603008 | tf_op jit(solution)/shard_map/all_gather | solution.py:14
  13.1 238.8 %all-gather.9.cloned.1.call-start = ((), (), s32[]{:S(2)}) async-start(), calls=%async_computation.1 | async-start | bytes 5242880 | tf_op jit(solution)/shard_map/all_gather | solution.py:22
  13.8 359.3 %all-gather.7.cloned.1.call-start = ((), (), s32[]{:S(2)}) async-start(), calls=%async_computation | async-start | bytes 9437184 | tf_op jit(solution)/shard_map/all_gather | solution.py:24
  17.7 551.7 %all-gather.13.cloned.1.call-start = ((), (), s32[]{:S(2)}) async-start(), calls=%async_computation.3 | async-start | bytes 34603008 | tf_op jit(solution)/shard_map/all_gather | solution.py:14
  240.0 7.5 %copy-start.1 = (bf16[1024,512]{1,0:T(8,128)(2,1)S(1)}, bf16[1024,512]{1,0:T(8,128)(2,1)}, u32[]{:S(2)}) copy-start(bf16[1024,512]{1,0:T(8,128)(2,1)} %multiply_convert_fusion) | copy-start | bytes 3145732
  240.0 7.5 %copy-start.2 = (f32[512,256]{1,0:T(8,128)S(1)}, f32[512,256]{1,0:T(8,128)}, u32[]{:S(2)}) copy-start(f32[512,256]{1,0:T(8,128)} %param.6) | copy-start | bytes 1572868
  240.1 8.8 %copy-start = (bf16[1024,512]{1,0:T(8,128)(2,1)S(1)}, bf16[1024,512]{1,0:T(8,128)(2,1)}, u32[]{:S(2)}) copy-start(bf16[1024,512]{1,0:T(8,128)(2,1)} %param.4) | copy-start | bytes 3145732
Sparse Core Ops, SparseCore 0:
  13.2 198.0 all-gather.10
  212.8 32.6 all-gather.8
  248.1 124.9 all-gather.6
  375.9 193.4 all-gather.12

commit v2 on v0

--- a/solution.py
+++ b/solution.py
@@ -37,7 +37,7 @@
         projected = jnp.dot(
             activations.astype(jnp.float32), change_now, precision=lax.Precision.HIGHEST
         )
-        totals = lax.psum(projected, ("row", "col"))
+        totals = jax.lax.psum(jax.lax.psum(projected, "col"), "row")
         pulled = lax.dot_general(
             weighted.astype(jnp.float32),
             totals,

time: 427 us -> 455 us (1.066)
  waiting for transfers between devices: 368 us -> 398 us
    psum x2 -> x4, waiting for transfers between devices: 367 us -> 237 us  [shards(): totals = jax.lax.psum(jax.lax.psum(projected, 'col'), 'row')]
    all_gather x1, waiting for transfers between devices: 0.01 us -> 127 us  [shards(): lax.all_gather(weighted, 'row', axis=1, tiled=True)]
    all_gather x1, waiting for transfers between devices: 0.01 us -> 31.9 us  [shards(): column_panel = lax.all_gather(activations, 'col', axis=1, tiled=True)]
  transfers between devices with their start and end apart: 4 -> 6, of which waited for: 2 -> 6; matrix products, arithmetic and copies ran while one was open for 1% -> 1% of each run, Pallas kernels for 0% -> 0%
where the time goes in v2:
time: 455 us
  waiting for transfers between devices  398 us (87%)
  matrix products  41.2 us (9%)
  between operations  14.2 us (3%)
    psum x4, waiting for transfers between devices, shards(): totals = jax.lax.psum(jax.lax.psum(projected, 'col'), 'row')  237 us
    all_gather x1, waiting for transfers between devices, shards(): lax.all_gather(weighted, 'row', axis=1, tiled=True)  127 us
    all_gather x1, waiting for transfers between devices, shards(): column_panel = lax.all_gather(activations, 'col', axis=1, tiled=True)  31.9 us
    dot_general x1, matrix products, shards(): lax.dot_general(lax.all_gather(weighted, 'row', axis=1, tiled=True), colu...  25.8 us
  transfers between devices with their start and end apart: 6, of which 6 were waited for; matrix products, arithmetic and copies ran while one was open for 1% of the time, Pallas kernels for 0%

profile of v2, /device:TPU:0, one launch (start us, length us, event | category | flops | bytes accessed | tf_op | source)
XLA Modules:
  0.0 455.0 jit_solution(9968012478435341155)
XLA Ops:
  7.2 0.0 copy-start
  7.2 0.0 copy-start.2
  7.2 0.0 all-reduce.5.cloned.1.call-start
  7.3 1.1 fusion.8
  8.3 0.6 broadcast_in_dim.2
  8.9 4.2 convolution_bitcast_fusion.1
  13.2 0.0 all-reduce.5.cloned.1.call-update
  13.2 0.0 all-reduce.7.cloned.1.call-start
  13.2 39.1 %all-reduce.5.cloned.1.call-done = f32[1024,256]{0,1:T(8,128)} async-done(((f32[1024,256]{0,1:T(8,128)}), f32[1024,256]{0,1:T(8,128)}) %all-reduce.5.cloned.1.call-update) | async-done | bytes 1048592 | tf_op jit(solution)/shard_map/psum | solution.py:40
  52.4 0.0 all-reduce.7.cloned.1.call-update
  52.4 0.0 all-reduce.9.cloned.1.call-start
  52.4 0.0 copy-done.2
  52.4 0.5 convert_reduce_fusion
  53.0 0.0 copy-done
  53.0 0.3 multiply_convert_fusion
  53.3 0.0 copy-start.1
  53.3 81.4 %all-reduce.7.cloned.1.call-done = f32[1024,256]{0,1:T(8,128)} async-done(((f32[1024,256]{0,1:T(8,128)}), f32[1024,256]{0,1:T(8,128)}) %all-reduce.7.cloned.1.call-update) | async-done | bytes 1048592 | tf_op jit(solution)/shard_map/psum | solution.py:40
  134.7 2.6 fusion.1
  137.3 3.9 convolution_bitcast_fusion
  141.2 0.0 all-reduce.9.cloned.1.call-update
  141.2 0.0 all-reduce.11.cloned.1.call-start
  141.3 36.0 %all-reduce.9.cloned.1.call-done = f32[1024,256]{0,1:T(8,128)} async-done(((f32[1024,256]{0,1:T(8,128)}), f32[1024,256]{0,1:T(8,128)}) %all-reduce.9.cloned.1.call-update) | async-done | bytes 1048592 | tf_op jit(solution)/shard_map/psum | solution.py:40
  177.2 0.0 all-reduce.11.cloned.1.call-update
  177.3 0.0 copy-done.1
  177.3 0.0 all-gather.5.cloned.1.call-start
  177.3 0.5 all-gather.5.cloned.1.call-update
  177.9 0.2 all-gather.3.cloned.1.call-start
  178.1 0.3 all-gather.3.cloned.1.call-update
  178.4 81.0 %all-reduce.11.cloned.1.call-done = f32[1024,256]{0,1:T(8,128)} async-done(((f32[1024,256]{0,1:T(8,128)}), f32[1024,256]{0,1:T(8,128)}) %all-reduce.11.cloned.1.call-update) | async-done | bytes 1048592 | tf_op jit(solution)/shard_map/psum | solution.py:40
  259.4 3.6 fusion.3
  263.0 31.9 %all-gather.5.cloned.1.call-done = bf16[1024,2048]{1,0:T(8,128)(2,1)} async-done(((bf16[1024,512]{1,0:T(8,128)(2,1)}), bf16[1024,2048]{1,0:T(8,128)(2,1)}) %all-gather.5.cloned.1.call-update) | async-done | bytes 4194320 | tf_op jit(solution)/shard_map/all_gather | solution.py:17
  294.9 127.4 %all-gather.3.cloned.1.call-done = bf16[1024,4096]{1,0:T(8,128)(2,1)} async-done(((bf16[1024,512]{1,0:T(8,128)(2,1)}), bf16[1024,4096]{1,0:T(8,128)(2,1)}) %all-gather.3.cloned.1.call-update) | async-done | bytes 8388624 | tf_op jit(solution)/shard_map/all_gather | solution.py:19
  422.3 25.8 %convolution_multiply_fusion = f32[4096,2048]{1,0:T(8,128)} fusion(bf16[1024,4096]{1,0:T(8,128)(2,1)} %all-gather.3.cloned.1.call-done, bf16[1024,2048]{1,0:T(8,128)(2,1)} %all-gather.5.cloned.1.call-done), kind=kOutput, calls=%fused_computation | convolution fusion | flops 17188257792 | bytes 46137344 | tf_op jit(solution)/shard_map/dot_general | solution.py:18
  (2 shorter events, 0.0 us)
Async XLA Ops:
  7.2 45.8 %copy-start = (bf16[1024,512]{1,0:T(8,128)(2,1)S(1)}, bf16[1024,512]{1,0:T(8,128)(2,1)}, u32[]{:S(2)}) copy-start(bf16[1024,512]{1,0:T(8,128)(2,1)} %param.4) | copy-start | bytes 3145732
  7.2 45.3 %copy-start.2 = (s32[1024]{0:T(1024)S(1)}, s32[1024]{0:T(1024)}, u32[]{:S(2)}) copy-start(s32[1024]{0:T(1024)} %param.5) | copy-start | bytes 12292
  7.2 45.2 %all-reduce.5.cloned.1.call-start = ((), (), s32[]{:S(2)}) async-start(), calls=%async_computation.2 | async-start | bytes 2097152 | tf_op jit(solution)/shard_map/psum | solution.py:40
  13.2 121.5 %all-reduce.7.cloned.1.call-start = ((), (), s32[]{:S(2)}) async-start(), calls=%async_computation.3 | async-start | bytes 2097152 | tf_op jit(solution)/shard_map/psum | solution.py:40
  52.4 124.9 %all-reduce.9.cloned.1.call-start = ((), (), s32[]{:S(2)}) async-start(), calls=%async_computation.4 | async-start | bytes 2097152 | tf_op jit(solution)/shard_map/psum | solution.py:40
  53.3 124.0 %copy-start.1 = (bf16[1024,512]{1,0:T(8,128)(2,1)}, bf16[1024,512]{1,0:T(8,128)(2,1)S(1)}, u32[]{:S(2)}) copy-start(bf16[1024,512]{1,0:T(8,128)(2,1)S(1)} %multiply_convert_fusion) | copy-start | bytes 3145732
  141.2 118.2 %all-reduce.11.cloned.1.call-start = ((), (), s32[]{:S(2)}) async-start(), calls=%async_computation.5 | async-start | bytes 2097152 | tf_op jit(solution)/shard_map/psum | solution.py:40
  177.3 117.6 %all-gather.5.cloned.1.call-start = ((), (), s32[]{:S(2)}) async-start(), calls=%async_computation.1 | async-start | bytes 5242880 | tf_op jit(solution)/shard_map/all_gather | solution.py:17
  177.9 244.5 %all-gather.3.cloned.1.call-start = ((), (), s32[]{:S(2)}) async-start(), calls=%async_computation | async-start | bytes 9437184 | tf_op jit(solution)/shard_map/all_gather | solution.py:19
Sparse Core Ops, SparseCore 0:
  13.3 39.0 all-reduce.4
  55.9 78.7 all-reduce.6
  141.3 35.8 all-reduce.8
  180.6 78.7 all-reduce.10
  260.8 34.0 all-gather.4
  297.4 124.9 all-gather.2
